TPU v7x, 128 devices: a whole 4x4x4 slice. The times are simulated.
128 devices in a mesh: wide: 32 (over z, y, x_hi), narrow: 4 (over x_lo, core).
Axes of the slice: x: 4 (x_hi: 2, x_lo: 2; x = x_hi * 2 + x_lo), y: 4, z: 4, core: 2. Of those that a mesh axis runs over, the one named last changes fastest.
Arguments:
- control: bfloat16 [512, 2, 512, 512], P('wide', None, None, 'narrow'), may hold values from -6 to 6
- legendre: bfloat16 [512, 512, 512], P('wide'), may hold values from -0.25 to 0.25
- loc_spectrum: float32 [512, 512], P('wide'), may hold values from 0.02 to 0.2
- ensemble: bfloat16 [512, 512, 1024], P('wide', 'narrow'), may hold values from -0.29882812 to 0.29882812
- order_map: int32 [512], replicated, may hold values from 0 to 511, each once
- obs_level: int32 [512, 256], P('wide'), may hold values from 0 to 7
- obs_lon: int32 [512, 256], P('wide'), may hold values from 0 to 1023
- obs_value: float32 [512, 256], P('wide'), may hold values from -12 to 12
- obs_weight: float32 [512, 256], P('wide'), may hold values from 2 to 40
Outputs:
- gradient: float32 [512, 2, 512, 512], P('wide', None, None, 'narrow')
Inputs may be any that keep to these rules, and one draw needn't show every extreme that they name: order_map is a permutation of the orders 0 to 511. `obs_lon`: several observations may share a grid point.
All inputs are finite; a program needn't handle non-finite values.
Results may differ from a plain program's by a relative error of at most 0.0057.
Values may be sent and summed in bfloat16 or wider, within the bound.
No kernel may reach another device: no remote copies, remote signals or barrier semaphores. Data moves between devices by JAX's collectives and lax.ppermute only.
A program may use at most 128 MiB of HBM per device.

v0:
```python
import jax
import jax.numpy as jnp
from jax import lax
from jax.experimental import pallas as pl
from jax.experimental.pallas import tpu as pltpu
from jax.sharding import PartitionSpec as P


LEVELS = 8
ROWS = 16
PLANES = 18
PICK = 4
ORDERS = 2
BLOCKS = 2
PITCH = 33
SIN = (6.2831851595779975, -41.34165492085311, 81.60099762205961, -76.54964290998956, 39.53570242643394)
COS = (0.9999999532360554, -19.739171315085017, 64.93458093602055, -85.24007915837501, 56.24034662339592)
HALF_SIN = tuple(2**0.5 * c / 2 ** (2 * i + 1) for i, c in enumerate(SIN))
HALF_COS = tuple(-(2**0.5) * c / 4**i for i, c in enumerate(COS))


def params(mib):
    return pltpu.CompilerParams(vmem_limit_bytes=mib * 2**20)


def in_hbm(x):
    return pltpu.with_memory_space_constraint(x, pltpu.HBM)


def horner(coefs, x):
    total = jnp.full_like(x, coefs[-1])
    for c in coefs[-2::-1]:
        total = total * x + c
    return total


def pick_kernel(level_ref, lon_ref, ens_ref, out_ref):
    b0 = pl.program_id(0) * PICK

    @pl.when(b0 == 0)
    def _():
        lon = lon_ref[...]
        out_ref[16] = (lon >> 3).astype(jnp.float32).astype(jnp.bfloat16)
        out_ref[17] = ((lon & 7) * LEVELS + level_ref[...]).astype(jnp.float32).astype(jnp.bfloat16)

    members, nobs = out_ref.shape[1], out_ref.shape[2]
    lons = ens_ref.shape[2]
    step = 256
    place = lax.broadcasted_iota(jnp.int32, (step, nobs), 0).astype(jnp.float32)
    place = place.astype(jnp.bfloat16)
    shape = (members, ens_ref.shape[1])
    same = lax.broadcasted_iota(jnp.int32, shape, 1) // LEVELS
    same = (same == lax.broadcasted_iota(jnp.int32, shape, 0)).astype(jnp.float32)
    same = same.astype(jnp.bfloat16)
    for k in range(PICK):
        lon = lon_ref[pl.ds(b0 + k, 1), :]
        level = level_ref[pl.ds(b0 + k, 1), :]
        onehot = []
        for s in range(0, lons, step):
            away = jnp.broadcast_to((lon - s).astype(jnp.float32), (16, nobs)).astype(jnp.bfloat16)
            away = jnp.concatenate([away] * (step // 16), axis=0)
            onehot.append(jnp.where(place == away, jnp.bfloat16(1), jnp.bfloat16(0)))
        total = jnp.dot(
            ens_ref[k], jnp.concatenate(onehot, axis=0), preferred_element_type=jnp.float32
        )
        mine = lax.broadcasted_iota(jnp.int32, (LEVELS, nobs), 0) == level
        total = jnp.where(mine[None], total.reshape(members, LEVELS, nobs), 0.0)
        total = total.reshape(members * LEVELS, nobs).astype(jnp.bfloat16)
        out_ref[b0 + k] = jnp.dot(same, total, preferred_element_type=jnp.float32).astype(
            jnp.bfloat16
        )


def pick(obs_level, obs_lon, ensemble):
    rows, width, lons = ensemble.shape
    nobs = obs_lon.shape[1]
    whole = pl.BlockSpec((rows, nobs), lambda b: (0, 0))
    return pl.pallas_call(
        pick_kernel,
        grid=(rows // PICK,),
        in_specs=[whole, whole, pl.BlockSpec((PICK, width, lons), lambda b: (b, 0, 0))],
        out_specs=pl.BlockSpec((PLANES, rows, nobs), lambda b: (0, 0, 0)),
        out_shape=jax.ShapeDtypeStruct((PLANES, rows, nobs), jnp.bfloat16),
        compiler_params=params(12),
        name="pick",
    )(in_hbm(obs_level), in_hbm(obs_lon), in_hbm(ensemble))


def order_of(order_ref, place_ref, m):
    return order_ref[((place_ref[0] * 4 + place_ref[1]) * 2 + place_ref[2]) * ROWS + m]


def column(loc_ref, m, order):
    row = loc_ref[pl.ds(m, 1), :]
    row = jnp.where(order == 0, row, row * 2.0)
    return jnp.broadcast_to(row, (128, row.shape[1])).T


def legendre_kernel(order_ref, place_ref, leg_ref, control_ref, loc_ref, out_ref, acc_ref):
    step = pl.program_id(0)
    lats = out_ref.shape[0]
    width = control_ref.shape[3]
    for k in range(ORDERS):
        m = step * ORDERS + k
        loc = column(loc_ref, m, order_of(order_ref, place_ref, m))
        scaled = [
            (control_ref[k, c].astype(jnp.float32) * loc).astype(jnp.bfloat16) for c in range(2)
        ]
        got = lax.dot_general(
            leg_ref[k],
            jnp.concatenate(scaled, axis=1),
            (((0,), (0,)), ((), ())),
            preferred_element_type=jnp.float32,
        )
        for c in range(2):
            acc_ref[pl.ds(c * ROWS + m, lats, stride=PITCH), :] = got[
                :, c * width : (c + 1) * width
            ]

    @pl.when(step == pl.num_programs(0) - 1)
    def _():
        def move(i, carry):
            for k in range(16):
                b = i * 16 + k
                out_ref[b] = acc_ref[pl.ds(b * PITCH, 2 * ROWS), :].astype(jnp.bfloat16)
            return carry

        lax.fori_loop(0, lats // 16, move, 0)


def legendre_forward(order_map, where, legendre, control, loc):
    slots, _, degs, width = control.shape
    lats = legendre.shape[2]
    return pl.pallas_call(
        legendre_kernel,
        grid_spec=pltpu.PrefetchScalarGridSpec(
            num_scalar_prefetch=2,
            grid=(slots // ORDERS,),
            in_specs=[
                pl.BlockSpec((ORDERS, degs, lats), lambda m, *_: (m, 0, 0)),
                pl.BlockSpec((ORDERS, 2, degs, width), lambda m, *_: (m, 0, 0, 0)),
                pl.BlockSpec((slots, degs), lambda m, *_: (0, 0)),
            ],
            out_specs=pl.BlockSpec((lats, 2 * slots, width), lambda m, *_: (0, 0, 0)),
            scratch_shapes=[pltpu.VMEM((lats * PITCH, width), jnp.float32)],
        ),
        out_shape=jax.ShapeDtypeStruct((lats, 2 * slots, width), jnp.bfloat16),
        compiler_params=params(22),
        cost_estimate=pl.CostEstimate(
            flops=2 * slots * degs * lats * 2 * width, bytes_accessed=16 * 2**20, transcendentals=0
        ),
        name="legendre_forward",
    )(order_map, where, in_hbm(legendre), in_hbm(control), in_hbm(loc))


def forward_kernel(order_ref, place_ref, e_ref, coeff_ref, *rest):
    part_ref, four_ref, keep_ref, lon_ref, lev_ref, ens_ref, sum_ref, turn_ref = rest[-8:]
    hi = e_ref[0, 16].astype(jnp.float32)
    lo = e_ref[0, 17].astype(jnp.float32)
    low = jnp.floor(lo * (1.0 / LEVELS))
    lon_ref[...] = hi * 8.0 + low
    lev_ref[...] = lo - low * LEVELS
    keep_ref[0] = e_ref[0]
    members, nobs = e_ref.shape[2], e_ref.shape[3]
    ens_ref[...] = e_ref[0, :ROWS].astype(jnp.float32)

    @pl.when(pl.program_id(0) == 0)
    def _():
        row = lax.broadcasted_iota(jnp.int32, turn_ref.shape, 0)
        order = jnp.zeros(turn_ref.shape, jnp.float32)
        for m in range(ROWS):
            order = jnp.where(
                row == m, order_of(order_ref, place_ref, m).astype(jnp.float32), order
            )
        turn_ref[...] = order * (1.0 / 1024.0)

    turn = turn_ref[...]
    grid_level = lax.broadcasted_iota(jnp.int32, (LEVELS, nobs), 0).astype(jnp.float32)

    def one(b):
        turns = turn * lon_ref[pl.ds(b, 1), :]
        frac = turns - jnp.floor(turns + 0.5)
        square = frac * frac
        sine = frac * horner(HALF_SIN, square)
        cosine = horner(HALF_COS, square)
        four = jnp.concatenate(
            [(1.0 - sine * sine).astype(jnp.bfloat16), (sine * cosine).astype(jnp.bfloat16)],
            axis=0,
        )
        four_ref[0, b] = four
        field = lax.dot_general(
            coeff_ref[b], four, (((0,), (0,)), ((), ())), preferred_element_type=jnp.float32
        )
        total = None
        for k in range(members):
            ens = ens_ref[b, k : k + 1]
            term = field[k * LEVELS : (k + 1) * LEVELS] * ens
            total = term if total is None else total + term
        mine = grid_level == lev_ref[pl.ds(b, 1), :]
        total = jnp.sum(jnp.where(mine, total, 0.0), axis=0, keepdims=True)
        for lane in range(0, nobs, 128):
            sum_ref[pl.ds((b * nobs + lane) // 128, 1), :] = total[:, lane : lane + 128]

    for b in range(ROWS):
        one(b)
    part_ref[...] = sum_ref[...].astype(jnp.bfloat16)


def forward(order_map, where, far, e, coeff, before):
    n = e.shape[0]
    lats, modes, width = coeff.shape
    nobs = e.shape[3]
    blocks = lats // ROWS
    lanes = nobs // 128

    def block(i, place):
        near = i >> 1
        turn = (far - near) * place[3]
        z, y = place[0] - far + turn, place[1] - near - turn
        return (z & 3) * 8 + (y & 3) * 2 + ((place[2] + i) & 1)

    e_spec = lambda f: pl.BlockSpec((1, PLANES, ROWS, nobs), f)
    at_block = lambda i, _, place: (block(i, place), 0, 0, 0)
    out_shape = (
        jax.ShapeDtypeStruct((lats * lanes, 128), jnp.bfloat16),
        jax.ShapeDtypeStruct((blocks, ROWS, modes, nobs), jnp.bfloat16),
        jax.ShapeDtypeStruct((blocks, PLANES, ROWS, nobs), jnp.bfloat16),
    )
    passed = () if before is None else tuple(before)
    return pl.pallas_call(
        forward_kernel,
        grid_spec=pltpu.PrefetchScalarGridSpec(
            num_scalar_prefetch=2,
            grid=(n,),
            in_specs=[
                e_spec(lambda i, _, place: (i, 0, 0, 0)),
                pl.BlockSpec((ROWS, modes, width), lambda i, _, place: (block(i, place), 0, 0)),
            ]
            + [pl.BlockSpec(memory_space=pl.ANY)] * len(passed),
            out_specs=(
                pl.BlockSpec((ROWS * lanes, 128), lambda i, _, place: (block(i, place), 0)),
                pl.BlockSpec((1, ROWS, modes, nobs), at_block),
                e_spec(at_block),
            ),
            scratch_shapes=[
                pltpu.VMEM((ROWS, nobs), jnp.float32),
                pltpu.VMEM((ROWS, nobs), jnp.float32),
                pltpu.VMEM((ROWS, ROWS, nobs), jnp.float32),
                pltpu.VMEM((ROWS * lanes, 128), jnp.float32),
                pltpu.VMEM((ROWS, nobs), jnp.float32),
            ],
        ),
        out_shape=out_shape,
        input_output_aliases={4 + i: i for i in range(len(passed))},
        compiler_params=params(6),
        cost_estimate=pl.CostEstimate(
            flops=n * 6 * 10**8, bytes_accessed=n * 2**19, transcendentals=0
        ),
        name="observe",
    )(order_map, where, e, coeff, *passed)


def backward_kernel(
    order_ref, place_ref, e_ref, four_ref, misfit_ref, leg_ref, control_ref, loc_ref, out_ref,
    back_ref, lev_ref, ens_ref, misfit32_ref,
):
    step = pl.program_id(0)
    nobs = e_ref.shape[3]
    members = e_ref.shape[2]
    modes = four_ref.shape[2]
    lats = back_ref.shape[0] // PITCH
    width = control_ref.shape[3]
    steps = lats // (ROWS * BLOCKS)

    @pl.when(step < steps)
    def _():
        misfit32_ref[...] = misfit_ref[...].astype(jnp.float32)
        grid_level = lax.broadcasted_iota(jnp.int32, (LEVELS, nobs), 0).astype(jnp.float32)
        for g in range(BLOCKS):
            lo = e_ref[g, 17].astype(jnp.float32)
            lev_ref[g] = lo - jnp.floor(lo * (1.0 / LEVELS)) * LEVELS
            for b in range(ROWS):
                row = (g * ROWS + b) * nobs // 128
                misfit = jnp.concatenate(
                    [
                        jnp.broadcast_to(misfit32_ref[row + lane : row + lane + 1], (members, 128))
                        for lane in range(nobs // 128)
                    ],
                    axis=1,
                )
                ens_ref[g, b] = e_ref[g, b].astype(jnp.float32) * misfit
            for b in range(ROWS):
                mine = grid_level == lev_ref[g, b : b + 1]
                spread = [
                    jnp.where(mine, ens_ref[g, b, k : k + 1], 0.0) for k in range(members)
                ]
                lat = (step * BLOCKS + g) * ROWS + b
                back_ref[pl.ds(lat * PITCH, modes), :] = lax.dot_general(
                    four_ref[g, b],
                    jnp.concatenate(spread, axis=0).astype(jnp.bfloat16),
                    (((1,), (1,)), ((), ())),
                    preferred_element_type=jnp.float32,
                )

    @pl.when(step >= steps)
    def _():
        for k in range(ORDERS):
            m = (step - steps) * ORDERS + k
            pieces = [
                back_ref[pl.ds(c * ROWS + m, lats, stride=PITCH), :].astype(jnp.bfloat16)
                for c in range(2)
            ]
            got = jnp.dot(
                leg_ref[k], jnp.concatenate(pieces, axis=1), preferred_element_type=jnp.float32
            )
            loc = column(loc_ref, m, order_of(order_ref, place_ref, m))
            for c in range(2):
                out_ref[k, c] = (
                    control_ref[k, c].astype(jnp.float32)
                    + loc * got[:, c * width : (c + 1) * width]
                )


def backward(order_map, where, e, four, misfit, legendre, control, loc):
    blocks, _, _, nobs = e.shape
    modes = four.shape[2]
    slots, _, degs, width = control.shape
    lats = legendre.shape[2]
    lanes = nobs // 128
    steps = blocks // BLOCKS
    first = lambda s: jnp.minimum(s, steps - 1)
    second = lambda s: jnp.maximum(s - steps, 0)
    per_slot = pl.BlockSpec((ORDERS, 2, degs, width), lambda s, *_: (second(s), 0, 0, 0))
    return pl.pallas_call(
        backward_kernel,
        grid_spec=pltpu.PrefetchScalarGridSpec(
            num_scalar_prefetch=2,
            grid=(steps + slots // ORDERS,),
            in_specs=[
                pl.BlockSpec((BLOCKS, PLANES, ROWS, nobs), lambda s, *_: (first(s), 0, 0, 0)),
                pl.BlockSpec((BLOCKS, ROWS, modes, nobs), lambda s, *_: (first(s), 0, 0, 0)),
                pl.BlockSpec((BLOCKS * ROWS * lanes, 128), lambda s, *_: (first(s), 0)),
                pl.BlockSpec((ORDERS, degs, lats), lambda s, *_: (second(s), 0, 0)),
                per_slot,
                pl.BlockSpec((slots, degs), lambda s, *_: (0, 0)),
            ],
            out_specs=per_slot,
            scratch_shapes=[
                pltpu.VMEM((lats * PITCH, width), jnp.float32),
                pltpu.VMEM((BLOCKS, ROWS, nobs), jnp.float32),
                pltpu.VMEM((BLOCKS, ROWS, ROWS, nobs), jnp.float32),
                pltpu.VMEM((BLOCKS * ROWS * lanes, 128), jnp.float32),
            ],
        ),
        out_shape=jax.ShapeDtypeStruct(control.shape, jnp.float32),
        compiler_params=params(24),
        name="adjoint",
    )(order_map, where, e, four, misfit, in_hbm(legendre), in_hbm(control), in_hbm(loc))


def send(x, distance, stage):
    pairs = []
    for w in range(32):
        for n in range(4):
            z, y, h = w // 8, w // 2 % 4, w % 2
            if stage == "hop":
                h = (h + distance) % 2
            elif (stage == "near") == (n % 2 == 0):
                y = (y + distance) % 4
            else:
                z = (z + distance) % 4
            pairs.append((w * 4 + n, (z * 8 + y * 2 + h) * 4 + n))
    return lax.ppermute(x, ("wide", "narrow"), pairs)


def gather(own):
    pair = jnp.concatenate([own, send(own, 1, "hop")], axis=0)
    near = [pair] + [send(pair, k, "near") for k in (1, 2, 3)]
    near = jnp.concatenate(near, axis=0)
    return [near] + [send(near, k, "far") for k in (1, 2, 3)]


def body(
    control, legendre, loc_spectrum, ensemble, order_map, obs_level, obs_lon, obs_value, obs_weight
):
    nobs = obs_lon.shape[1]
    both = ("wide", "narrow")
    devices = lax.axis_size(both)
    mine = obs_lon.shape[0] * lax.axis_size("wide") // devices
    tile = mine * nobs // 128
    w = lax.axis_index("wide")
    n = lax.axis_index("narrow")
    where = jnp.stack([w >> 3, (w >> 1) & 3, w & 1, n & 1]).astype(jnp.int32)
    own = pick(obs_level, obs_lon, ensemble)

    blocks = gather(own)

    coeff = legendre_forward(order_map, where, legendre, control, loc_spectrum)
    state = None
    for far in (0, 1, 3, 2):
        e = blocks[far].reshape(-1, PLANES, ROWS, nobs)
        state = forward(order_map, where, far, e, coeff, state)
    part, four, e_all = state

    value = lax.dynamic_slice_in_dim(obs_value, n * mine, mine, 0).reshape(tile, 128)
    weight = lax.dynamic_slice_in_dim(obs_weight, n * mine, mine, 0).reshape(tile, 128)
    part, value, weight = lax.optimization_barrier((part, value, weight))
    parts = lax.all_to_all(
        part.reshape(devices, tile, 128), both, split_axis=0, concat_axis=0, tiled=True
    )
    picked = jnp.sum(parts.astype(jnp.float32), axis=0)
    misfit = (weight * (picked - value)).astype(jnp.bfloat16)
    misfit = jnp.broadcast_to(misfit[None], (devices, tile, 128))
    misfit = lax.all_to_all(misfit, both, split_axis=0, concat_axis=0, tiled=True)
    misfit = misfit.reshape(part.shape)
    return backward(order_map, where, e_all, four, misfit, legendre, control, loc_spectrum)


def solution(mesh):
    rows = P("wide", None)
    return jax.shard_map(
        body,
        mesh=mesh,
        in_specs=(
            P("wide", None, None, "narrow"),
            P("wide", None, None),
            rows,
            P("wide", "narrow", None),
            P(),
            rows,
            rows,
            rows,
            rows,
        ),
        out_specs=P("wide", None, None, "narrow"),
        check_vma=False,
    )
```

profile of v0, /device:TPU:0, one launch (start us, length us, event | category | flops | bytes accessed | tf_op | source)
XLA Modules:
  0.0 124.4 jit_solution(11564303450504022721)
XLA Ops:
  0.0 5.4 %pick.1 = bf16[18,16,256]{2,1,0:T(8,128)(2,1)S(1)} custom-call(s32[16,256]{1,0:T(8,128)} %level_ref.1, s32[16,256]{1,0:T(8,128)} %lon_ref.1, bf16[16,128,1024]{2,1,0:T(8,128)(2,1)} %ens_ref.1), custom_call_target="tpu_custom_call" | custom-call | tf_op jit(solution)/shard_map/pick/pallas_call | solution.py:78
  5.4 3.1 %collective-permute-start = (bf16[18,16,256]{2,1,0:T(8,128)(2,1)S(1)}, bf16[18,16,256]{2,1,0:T(8,128)(2,1)S(1)}, u32[]{:S(2)}, u32[]{:S(2)}) collective-permute-start(bf16[18,16,256]{2,1,0:T(8,128)(2,1)S(1)} %pick.1), channel_id=1, source_target_pairs={{0,4},{1,5},{2,6},{3,7},{4,0},{5,1},{6,2},{7,3},{8,12},{9,13},{10,... | collective-permute-start | bytes 442376 | tf_op jit(solution)/shard_map/ppermute | solution.py:373
  8.6 3.8 %collective-permute-done = bf16[18,16,256]{2,1,0:T(8,128)(2,1)S(1)} collective-permute-done((bf16[18,16,256]{2,1,0:T(8,128)(2,1)S(1)}, bf16[18,16,256]{2,1,0:T(8,128)(2,1)S(1)}, u32[]{:S(2)}, u32[]{:S(2)}) %collective-permute-start) | collective-permute-done | bytes 147488 | tf_op jit(solution)/shard_map/ppermute | solution.py:373
  12.5 0.0 copy-start
  12.5 1.9 %collective-permute-start.1 = (bf16[36,16,256]{2,1,0:T(8,128)(2,1)S(1)}, bf16[36,16,256]{2,1,0:T(8,128)(2,1)S(1)}, u32[]{:S(2)}, u32[]{:S(2)}) collective-permute-start(bf16[36,16,256]{2,1,0:T(8,128)(2,1)S(1)} %pad_maximum_fusion), channel_id=1, source_target_pairs={{0,8},{1,33},{2,10},{3,35},{4,12},{5,37},{6,14},{7,39},{8,16},{9,4... | collective-permute-start | bytes 884744 | tf_op jit(solution)/shard_map/ppermute | solution.py:373
  14.4 2.9 %collective-permute-start.2 = (bf16[36,16,256]{2,1,0:T(8,128)(2,1)S(1)}, bf16[36,16,256]{2,1,0:T(8,128)(2,1)S(1)}, u32[]{:S(2)}, u32[]{:S(2)}) collective-permute-start(bf16[36,16,256]{2,1,0:T(8,128)(2,1)S(1)} %pad_maximum_fusion), channel_id=1, source_target_pairs={{0,16},{1,65},{2,18},{3,67},{4,20},{5,69},{6,22},{7,71},{8,24},{9,... | collective-permute-start | bytes 884744 | tf_op jit(solution)/shard_map/ppermute | solution.py:373
  17.3 1.4 %collective-permute-start.3 = (bf16[36,16,256]{2,1,0:T(8,128)(2,1)S(1)}, bf16[36,16,256]{2,1,0:T(8,128)(2,1)S(1)}, u32[]{:S(2)}, u32[]{:S(2)}) collective-permute-start(bf16[36,16,256]{2,1,0:T(8,128)(2,1)S(1)} %pad_maximum_fusion), channel_id=1, source_target_pairs={{0,24},{1,97},{2,26},{3,99},{4,28},{5,101},{6,30},{7,103},{8,0},{9... | collective-permute-start | bytes 884744 | tf_op jit(solution)/shard_map/ppermute | solution.py:373
  18.7 1.8 %collective-permute-done.1 = bf16[36,16,256]{2,1,0:T(8,128)(2,1)S(1)} collective-permute-done((bf16[36,16,256]{2,1,0:T(8,128)(2,1)S(1)}, bf16[36,16,256]{2,1,0:T(8,128)(2,1)S(1)}, u32[]{:S(2)}, u32[]{:S(2)}) %collective-permute-start.1) | collective-permute-done | bytes 294944 | tf_op jit(solution)/shard_map/ppermute | solution.py:373
  20.5 4.6 %collective-permute-done.2 = bf16[36,16,256]{2,1,0:T(8,128)(2,1)S(1)} collective-permute-done((bf16[36,16,256]{2,1,0:T(8,128)(2,1)S(1)}, bf16[36,16,256]{2,1,0:T(8,128)(2,1)S(1)}, u32[]{:S(2)}, u32[]{:S(2)}) %collective-permute-start.2) | collective-permute-done | bytes 294944 | tf_op jit(solution)/shard_map/ppermute | solution.py:373
  25.1 0.0 collective-permute-done.3
  25.2 2.0 %collective-permute-start.6 = (bf16[144,16,256]{2,1,0:T(8,128)(2,1)S(1)}, bf16[144,16,256]{2,1,0:T(8,128)(2,1)S(1)}, u32[]{:S(2)}, u32[]{:S(2)}) collective-permute-start(bf16[144,16,256]{2,1,0:T(8,128)(2,1)S(1)} %constant_dynamic-update-slice_fusion), channel_id=1, source_target_pairs={{0,32},{1,9},{2,34},{3,11},{4,36},{5,13},{6,38},{7,15},{8,40},{9,1... | collective-permute-start | bytes 3538952 | tf_op jit(solution)/shard_map/ppermute | solution.py:373
  27.2 0.7 constant_dynamic-slice_fusion
  27.9 2.2 %collective-permute-start.5 = (bf16[144,16,256]{2,1,0:T(8,128)(2,1)S(1)}, bf16[144,16,256]{2,1,0:T(8,128)(2,1)S(1)}, u32[]{:S(2)}, u32[]{:S(2)}) collective-permute-start(bf16[144,16,256]{2,1,0:T(8,128)(2,1)S(1)} %constant_dynamic-update-slice_fusion), channel_id=1, source_target_pairs={{0,96},{1,25},{2,98},{3,27},{4,100},{5,29},{6,102},{7,31},{8,104},... | collective-permute-start | bytes 3538952 | tf_op jit(solution)/shard_map/ppermute | solution.py:373
  30.1 0.1 pad_add_fusion.place_ref
  30.2 0.0 copy-done
  30.2 10.5 %legendre_forward.1.coeff_ref = bf16[512,32,128]{2,1,0:T(8,128)(2,1)S(1)} custom-call(s32[512]{0:T(512)S(1)} %copy-done, s32[4]{0:T(128)S(1)} %pad_add_fusion.place_ref, bf16[16,512,512]{2,1,0:T(8,128)(2,1)} %leg_ref.3, bf16[16,2,512,128]{3,2,1,0:T(8,128)(2,1)} %control_ref.3, f32[16,512]{1,0:T(8,128)} %loc_ref.3), custom_call_target="tpu_custom_call" | custom-call | flops 2147483648 | bytes 16777216 | tf_op jit(solution)/shard_map/legendre_forward/pallas_call | solution.py:134
  40.7 1.9 %collective-permute-start.4 = (bf16[144,16,256]{2,1,0:T(8,128)(2,1)S(1)}, bf16[144,16,256]{2,1,0:T(8,128)(2,1)S(1)}, u32[]{:S(2)}, u32[]{:S(2)}) collective-permute-start(bf16[144,16,256]{2,1,0:T(8,128)(2,1)S(1)} %constant_dynamic-update-slice_fusion), channel_id=1, source_target_pairs={{0,64},{1,17},{2,66},{3,19},{4,68},{5,21},{6,70},{7,23},{8,72},{9,... | collective-permute-start | bytes 3538952 | tf_op jit(solution)/shard_map/ppermute | solution.py:373
  42.6 5.0 %observe.4 = (bf16[1024,128]{1,0:T(8,128)(2,1)S(1)}, bf16[32,16,32,256]{3,2,1,0:T(8,128)(2,1)S(1)}, bf16[32,18,16,256]{3,2,1,0:T(8,128)(2,1)S(1)}) custom-call(s32[512]{0:T(512)S(1)} %copy-done, s32[4]{0:T(128)S(1)} %pad_add_fusion.place_ref, bf16[8,18,16,256]{3,2,1,0:T(8,128)(2,1)S(1)} %bitcast.15, bf16[512,32,128]{2,1,0:T(8,128)(2,1)S(1)} %legendre_forward.1.coeff_ref), custom_call_target="tpu_custom_call" | custom-call | flops 4800000000 | bytes 4194304 | tf_op jit(solution)/shard_map/observe/pallas_call | solution.py:230
  47.7 0.0 collective-permute-done.6
  47.7 5.0 %observe.5 = (bf16[1024,128]{1,0:T(8,128)(2,1)S(1)}, bf16[32,16,32,256]{3,2,1,0:T(8,128)(2,1)S(1)}, bf16[32,18,16,256]{3,2,1,0:T(8,128)(2,1)S(1)}) custom-call(s32[512]{0:T(512)S(1)} %copy-done, s32[4]{0:T(128)S(1)} %pad_add_fusion.place_ref, bf16[8,18,16,256]{3,2,1,0:T(8,128)(2,1)S(1)} %bitcast.11, ...), custom_call_target="tpu_custom_call", output_to_operand_aliasing={{0}: (4, {}), {1}: (5, {}), {2}: (6, {})} | custom-call | flops 4800000000 | bytes 4194304 | tf_op jit(solution)/shard_map/observe/pallas_call | solution.py:230
  52.7 0.0 collective-permute-done.5
  52.7 5.0 %observe.6 = (bf16[1024,128]{1,0:T(8,128)(2,1)S(1)}, bf16[32,16,32,256]{3,2,1,0:T(8,128)(2,1)S(1)}, bf16[32,18,16,256]{3,2,1,0:T(8,128)(2,1)S(1)}) custom-call(s32[512]{0:T(512)S(1)} %copy-done, s32[4]{0:T(128)S(1)} %pad_add_fusion.place_ref, bf16[8,18,16,256]{3,2,1,0:T(8,128)(2,1)S(1)} %bitcast.13, ...), custom_call_target="tpu_custom_call", output_to_operand_aliasing={{0}: (4, {}), {1}: (5, {}), {2}: (6, {})} | custom-call | flops 4800000000 | bytes 4194304 | tf_op jit(solution)/shard_map/observe/pallas_call | solution.py:230
  57.8 0.7 collective-permute-done.4
  58.5 5.0 %observe.7 = (bf16[1024,128]{1,0:T(8,128)(2,1)S(1)}, bf16[32,16,32,256]{3,2,1,0:T(8,128)(2,1)S(1)}, bf16[32,18,16,256]{3,2,1,0:T(8,128)(2,1)S(1)}) custom-call(s32[512]{0:T(512)S(1)} %copy-done, s32[4]{0:T(128)S(1)} %pad_add_fusion.place_ref, bf16[8,18,16,256]{3,2,1,0:T(8,128)(2,1)S(1)} %bitcast.12, ...), custom_call_target="tpu_custom_call", output_to_operand_aliasing={{0}: (4, {}), {1}: (5, {}), {2}: (6, {})} | custom-call | flops 4800000000 | bytes 4194304 | tf_op jit(solution)/shard_map/observe/pallas_call | solution.py:230
  63.5 20.0 %all_to_all.10 = bf16[128,8,128]{2,1,0:T(8,128)(2,1)S(1)} all-to-all(bf16[128,8,128]{2,1,0:T(8,128)(2,1)S(1)} %bitcast.10), channel_id=1, replica_groups=mesh['wide'=32,'narrow'=4] {'wide','narrow'}, dimensions={0} | all-to-all | bytes 524288 | tf_op jit(solution)/shard_map/all_to_all | solution.py:408
  83.6 0.1 convert_reduce_fusion
  83.8 15.3 %all_to_all.11 = bf16[128,8,128]{2,1,0:T(8,128)(2,1)S(1)} all-to-all(bf16[128,8,128]{2,1,0:T(8,128)(2,1)S(1)} %broadcast_in_dim.2), channel_id=1, replica_groups=mesh['wide'=32,'narrow'=4] {'wide','narrow'}, dimensions={0} | all-to-all | bytes 524288 | tf_op jit(solution)/shard_map/all_to_all | solution.py:414
  99.1 25.4 %adjoint.1 = f32[16,2,512,128]{3,2,1,0:T(8,128)} custom-call(s32[512]{0:T(512)S(1)} %copy-done, s32[4]{0:T(128)S(1)} %pad_add_fusion.place_ref, bf16[32,18,16,256]{3,2,1,0:T(8,128)(2,1)S(1)} %get-tuple-element.29.e_ref, bf16[32,16,32,256]{3,2,1,0:T(8,128)(2,1)S(1)} %get-tuple-element.30.four_ref, bf16[1024,128]{1,0:T(8,128)(2,1)S(1)} %bitcast.14, ...), custom_call_target="tpu_custom_call" | custom-call | tf_op jit(solution)/shard_map/adjoint/pallas_call | solution.py:334
  (10 shorter events, 0.2 us)
Async XLA Ops:
  5.4 7.0 %collective-permute-start = (bf16[18,16,256]{2,1,0:T(8,128)(2,1)S(1)}, bf16[18,16,256]{2,1,0:T(8,128)(2,1)S(1)}, u32[]{:S(2)}, u32[]{:S(2)}) collective-permute-start(bf16[18,16,256]{2,1,0:T(8,128)(2,1)S(1)} %pick.1), channel_id=1, source_target_pairs={{0,4},{1,5},{2,6},{3,7},{4,0},{5,1},{6,2},{7,3},{8,12},{9,13},{10,... | collective-permute-start | bytes 442376 | tf_op jit(solution)/shard_map/ppermute | solution.py:373
  12.5 17.7 %copy-start = (s32[512]{0:T(512)S(1)}, s32[512]{0:T(512)}, u32[]{:S(2)}) copy-start(s32[512]{0:T(512)} %order_ref.11) | copy-start | bytes 6148
  12.5 8.0 %collective-permute-start.1 = (bf16[36,16,256]{2,1,0:T(8,128)(2,1)S(1)}, bf16[36,16,256]{2,1,0:T(8,128)(2,1)S(1)}, u32[]{:S(2)}, u32[]{:S(2)}) collective-permute-start(bf16[36,16,256]{2,1,0:T(8,128)(2,1)S(1)} %pad_maximum_fusion), channel_id=1, source_target_pairs={{0,8},{1,33},{2,10},{3,35},{4,12},{5,37},{6,14},{7,39},{8,16},{9,4... | collective-permute-start | bytes 884744 | tf_op jit(solution)/shard_map/ppermute | solution.py:373
  14.4 10.8 %collective-permute-start.2 = (bf16[36,16,256]{2,1,0:T(8,128)(2,1)S(1)}, bf16[36,16,256]{2,1,0:T(8,128)(2,1)S(1)}, u32[]{:S(2)}, u32[]{:S(2)}) collective-permute-start(bf16[36,16,256]{2,1,0:T(8,128)(2,1)S(1)} %pad_maximum_fusion), channel_id=1, source_target_pairs={{0,16},{1,65},{2,18},{3,67},{4,20},{5,69},{6,22},{7,71},{8,24},{9,... | collective-permute-start | bytes 884744 | tf_op jit(solution)/shard_map/ppermute | solution.py:373
  17.3 7.9 %collective-permute-start.3 = (bf16[36,16,256]{2,1,0:T(8,128)(2,1)S(1)}, bf16[36,16,256]{2,1,0:T(8,128)(2,1)S(1)}, u32[]{:S(2)}, u32[]{:S(2)}) collective-permute-start(bf16[36,16,256]{2,1,0:T(8,128)(2,1)S(1)} %pad_maximum_fusion), channel_id=1, source_target_pairs={{0,24},{1,97},{2,26},{3,99},{4,28},{5,101},{6,30},{7,103},{8,0},{9... | collective-permute-start | bytes 884744 | tf_op jit(solution)/shard_map/ppermute | solution.py:373
  25.2 22.5 %collective-permute-start.6 = (bf16[144,16,256]{2,1,0:T(8,128)(2,1)S(1)}, bf16[144,16,256]{2,1,0:T(8,128)(2,1)S(1)}, u32[]{:S(2)}, u32[]{:S(2)}) collective-permute-start(bf16[144,16,256]{2,1,0:T(8,128)(2,1)S(1)} %constant_dynamic-update-slice_fusion), channel_id=1, source_target_pairs={{0,32},{1,9},{2,34},{3,11},{4,36},{5,13},{6,38},{7,15},{8,40},{9,1... | collective-permute-start | bytes 3538952 | tf_op jit(solution)/shard_map/ppermute | solution.py:373
  27.9 24.8 %collective-permute-start.5 = (bf16[144,16,256]{2,1,0:T(8,128)(2,1)S(1)}, bf16[144,16,256]{2,1,0:T(8,128)(2,1)S(1)}, u32[]{:S(2)}, u32[]{:S(2)}) collective-permute-start(bf16[144,16,256]{2,1,0:T(8,128)(2,1)S(1)} %constant_dynamic-update-slice_fusion), channel_id=1, source_target_pairs={{0,96},{1,25},{2,98},{3,27},{4,100},{5,29},{6,102},{7,31},{8,104},... | collective-permute-start | bytes 3538952 | tf_op jit(solution)/shard_map/ppermute | solution.py:373
  40.7 17.8 %collective-permute-start.4 = (bf16[144,16,256]{2,1,0:T(8,128)(2,1)S(1)}, bf16[144,16,256]{2,1,0:T(8,128)(2,1)S(1)}, u32[]{:S(2)}, u32[]{:S(2)}) collective-permute-start(bf16[144,16,256]{2,1,0:T(8,128)(2,1)S(1)} %constant_dynamic-update-slice_fusion), channel_id=1, source_target_pairs={{0,64},{1,17},{2,66},{3,19},{4,68},{5,21},{6,70},{7,23},{8,72},{9,... | collective-permute-start | bytes 3538952 | tf_op jit(solution)/shard_map/ppermute | solution.py:373
where the time goes:
time: 126 us; the launch traced here: 124 us
  Pallas kernels  61.5 us (49%)
  blocking collectives  35.3 us (28%)
  starting transfers between devices  15.4 us (12%)
  waiting for transfers between devices  10.9 us (9%)
    pallas_call x1, Pallas kernels, backward(): pl.pallas_call(backward_kernel, grid_spec=pltpu.PrefetchScalarGridSpec(nu...  25.4 us
    pallas_call x4, Pallas kernels, forward(): pl.pallas_call(forward_kernel, grid_spec=pltpu.PrefetchScalarGridSpec(num...  20.2 us
    all_to_all x1, blocking collectives, body(): lax.all_to_all(part.reshape(devices, tile, 128), both, split_axis=0, conc...  20 us
    ppermute x7, starting transfers between devices, send(): return lax.ppermute(x, ('wide', 'narrow'), pairs)  15.4 us
    all_to_all x1, blocking collectives, body(): lax.all_to_all(misfit, both, split_axis=0, concat_axis=0, tiled=True)  15.3 us
    ppermute x7, waiting for transfers between devices, send(): return lax.ppermute(x, ('wide', 'narrow'), pairs)  10.9 us
    pallas_call x1, Pallas kernels, legendre_forward(): pl.pallas_call(legendre_kernel, grid_spec=pltpu.PrefetchScalarGridSpec(nu...  10.5 us
    pallas_call x1, Pallas kernels, pick(): pl.pallas_call(pick_kernel, grid=(rows // PICK,), in_specs=[whole, whole,...  5.45 us
  transfers between devices with their start and end apart: 7, of which 4 were waited for; matrix products, arithmetic and copies ran while one was open for 1% of the time, Pallas kernels for 21%

commit v1 on v0

--- a/solution.py
+++ b/solution.py
@@ -48,10 +48,6 @@
     step = 256
     place = lax.broadcasted_iota(jnp.int32, (step, nobs), 0).astype(jnp.float32)
     place = place.astype(jnp.bfloat16)
-    shape = (members, ens_ref.shape[1])
-    same = lax.broadcasted_iota(jnp.int32, shape, 1) // LEVELS
-    same = (same == lax.broadcasted_iota(jnp.int32, shape, 0)).astype(jnp.float32)
-    same = same.astype(jnp.bfloat16)
     for k in range(PICK):
         lon = lon_ref[pl.ds(b0 + k, 1), :]
         level = level_ref[pl.ds(b0 + k, 1), :]
@@ -65,10 +61,7 @@
         )
         mine = lax.broadcasted_iota(jnp.int32, (LEVELS, nobs), 0) == level
         total = jnp.where(mine[None], total.reshape(members, LEVELS, nobs), 0.0)
-        total = total.reshape(members * LEVELS, nobs).astype(jnp.bfloat16)
-        out_ref[b0 + k] = jnp.dot(same, total, preferred_element_type=jnp.float32).astype(
-            jnp.bfloat16
-        )
+        out_ref[b0 + k] = jnp.sum(total, axis=1).astype(jnp.bfloat16)
 
 
 def pick(obs_level, obs_lon, ensemble):
@@ -206,7 +199,7 @@
     part_ref[...] = sum_ref[...].astype(jnp.bfloat16)
 
 
-def forward(order_map, where, far, e, coeff, before):
+def forward(order_map, where, plane, far, e, coeff, before):
     n = e.shape[0]
     lats, modes, width = coeff.shape
     nobs = e.shape[3]
@@ -214,10 +207,9 @@
     lanes = nobs // 128
 
     def block(i, place):
-        near = i >> 1
-        turn = (far - near) * place[3]
-        z, y = place[0] - far + turn, place[1] - near - turn
-        return (z & 3) * 8 + (y & 3) * 2 + ((place[2] + i) & 1)
+        turn = (far - i) * place[3]
+        z, y = place[0] - far + turn, place[1] - i - turn
+        return (z & 3) * 8 + (y & 3) * 2 + ((place[2] + plane) & 1)
 
     e_spec = lambda f: pl.BlockSpec((1, PLANES, ROWS, nobs), f)
     at_block = lambda i, _, place: (block(i, place), 0, 0, 0)
@@ -374,10 +366,13 @@
 
 
 def gather(own):
-    pair = jnp.concatenate([own, send(own, 1, "hop")], axis=0)
-    near = [pair] + [send(pair, k, "near") for k in (1, 2, 3)]
-    near = jnp.concatenate(near, axis=0)
-    return [near] + [send(near, k, "far") for k in (1, 2, 3)]
+    ring = (1, 3, 2)
+    near = {k: send(own, k, "near") for k in ring}
+    near = jnp.concatenate([own] + [near[k] for k in (1, 2, 3)], axis=0)
+    other = send(near, 1, "hop")
+    far = [(0, k, send(near, k, "far")) for k in ring]
+    across = [(1, k, send(other, k, "far")) for k in ring]
+    return [(0, 0, near)] + far + [(1, 0, other)] + across
 
 
 def body(
@@ -397,9 +392,9 @@
 
     coeff = legendre_forward(order_map, where, legendre, control, loc_spectrum)
     state = None
-    for far in (0, 1, 3, 2):
-        e = blocks[far].reshape(-1, PLANES, ROWS, nobs)
-        state = forward(order_map, where, far, e, coeff, state)
+    for plane, far, e in blocks:
+        e = e.reshape(-1, PLANES, ROWS, nobs)
+        state = forward(order_map, where, plane, far, e, coeff, state)
     part, four, e_all = state
 
     value = lax.dynamic_slice_in_dim(obs_value, n * mine, mine, 0).reshape(tile, 128)

time: 126 us -> 121 us (0.960)
  waiting for transfers between devices: 10.9 us -> 3.81 us
  starting transfers between devices: 15.4 us -> 18.9 us
  blocking collectives: 35.3 us -> 33.3 us
    ppermute x7 -> x10, waiting for transfers between devices: 10.9 us -> 3.81 us  [send(): return lax.ppermute(x, ('wide', 'narrow'), pairs)]
    ppermute x7 -> x10, starting transfers between devices: 15.4 us -> 18.9 us  [send(): return lax.ppermute(x, ('wide', 'narrow'), pairs)]
    pallas_call x4 -> x8, Pallas kernels: 20.2 us -> 22.5 us  [forward(): pl.pallas_call(forward_kernel, grid_spec=pltpu.PrefetchScalarGridSpec(num...]
    all_to_all x1, blocking collectives: 20 us -> 18 us  [body(): lax.all_to_all(part.reshape(devices, tile, 128), both, split_axis=0, conc...]
  transfers between devices with their start and end apart: 7 -> 10, of which waited for: 4 -> 3; matrix products, arithmetic and copies ran while one was open for 1% -> 1% of each run, Pallas kernels for 21% -> 25%
where the time goes in v1:
time: 121 us; the launch traced here: 120 us
  Pallas kernels  62.7 us (52%)
  blocking collectives  33.3 us (28%)
  starting transfers between devices  18.9 us (16%)
  waiting for transfers between devices  3.81 us (3%)
    pallas_call x1, Pallas kernels, backward(): pl.pallas_call(backward_kernel, grid_spec=pltpu.PrefetchScalarGridSpec(nu...  25.4 us
    pallas_call x8, Pallas kernels, forward(): pl.pallas_call(forward_kernel, grid_spec=pltpu.PrefetchScalarGridSpec(num...  22.5 us
    ppermute x10, starting transfers between devices, send(): return lax.ppermute(x, ('wide', 'narrow'), pairs)  18.9 us
    all_to_all x1, blocking collectives, body(): lax.all_to_all(part.reshape(devices, tile, 128), both, split_axis=0, conc...  18 us
    all_to_all x1, blocking collectives, body(): lax.all_to_all(misfit, both, split_axis=0, concat_axis=0, tiled=True)  15.3 us
    pallas_call x1, Pallas kernels, legendre_forward(): pl.pallas_call(legendre_kernel, grid_spec=pltpu.PrefetchScalarGridSpec(nu...  10.5 us
    pallas_call x1, Pallas kernels, pick(): pl.pallas_call(pick_kernel, grid=(rows // PICK,), in_specs=[whole, whole,...  4.3 us
    ppermute x10, waiting for transfers between devices, send(): return lax.ppermute(x, ('wide', 'narrow'), pairs)  3.81 us
  transfers between devices with their start and end apart: 10, of which 3 were waited for; matrix products, arithmetic and copies ran while one was open for 1% of the time, Pallas kernels for 25%

profile of v1, /device:TPU:0, one launch (start us, length us, event | category | flops | bytes accessed | tf_op | source)
XLA Modules:
  0.0 120.0 jit_solution(16906959024852699428)
XLA Ops:
  0.0 0.0 copy-start
  0.0 4.3 %pick.1 = bf16[18,16,256]{2,1,0:T(8,128)(2,1)S(1)} custom-call(s32[16,256]{1,0:T(8,128)} %level_ref.1, s32[16,256]{1,0:T(8,128)} %lon_ref.1, bf16[16,128,1024]{2,1,0:T(8,128)(2,1)} %ens_ref.1), custom_call_target="tpu_custom_call" | custom-call | tf_op jit(solution)/shard_map/pick/pallas_call | solution.py:71
  4.3 1.8 %collective-permute-start = (bf16[18,16,256]{2,1,0:T(8,128)(2,1)S(1)}, bf16[18,16,256]{2,1,0:T(8,128)(2,1)S(1)}, u32[]{:S(2)}, u32[]{:S(2)}) collective-permute-start(bf16[18,16,256]{2,1,0:T(8,128)(2,1)S(1)} %pick.1), channel_id=1, source_target_pairs={{0,8},{1,33},{2,10},{3,35},{4,12},{5,37},{6,14},{7,39},{8,16},{9,4... | collective-permute-start | bytes 442376 | tf_op jit(solution)/shard_map/ppermute | solution.py:365
  6.1 2.9 %collective-permute-start.1 = (bf16[18,16,256]{2,1,0:T(8,128)(2,1)S(1)}, bf16[18,16,256]{2,1,0:T(8,128)(2,1)S(1)}, u32[]{:S(2)}, u32[]{:S(2)}) collective-permute-start(bf16[18,16,256]{2,1,0:T(8,128)(2,1)S(1)} %pick.1), channel_id=1, source_target_pairs={{0,16},{1,65},{2,18},{3,67},{4,20},{5,69},{6,22},{7,71},{8,24},{9,... | collective-permute-start | bytes 442376 | tf_op jit(solution)/shard_map/ppermute | solution.py:365
  9.0 1.3 %collective-permute-start.2 = (bf16[18,16,256]{2,1,0:T(8,128)(2,1)S(1)}, bf16[18,16,256]{2,1,0:T(8,128)(2,1)S(1)}, u32[]{:S(2)}, u32[]{:S(2)}) collective-permute-start(bf16[18,16,256]{2,1,0:T(8,128)(2,1)S(1)} %pick.1), channel_id=1, source_target_pairs={{0,24},{1,97},{2,26},{3,99},{4,28},{5,101},{6,30},{7,103},{8,0},{9... | collective-permute-start | bytes 442376 | tf_op jit(solution)/shard_map/ppermute | solution.py:365
  10.3 0.4 collective-permute-done
  10.7 2.9 %collective-permute-done.1 = bf16[18,16,256]{2,1,0:T(8,128)(2,1)S(1)} collective-permute-done((bf16[18,16,256]{2,1,0:T(8,128)(2,1)S(1)}, bf16[18,16,256]{2,1,0:T(8,128)(2,1)S(1)}, u32[]{:S(2)}, u32[]{:S(2)}) %collective-permute-start.1) | collective-permute-done | bytes 147488 | tf_op jit(solution)/shard_map/ppermute | solution.py:365
  13.7 0.4 collective-permute-done.2
  14.1 0.1 pad_maximum_fusion
  14.2 2.0 %collective-permute-start.9 = (bf16[72,16,256]{2,1,0:T(8,128)(2,1)S(1)}, bf16[72,16,256]{2,1,0:T(8,128)(2,1)S(1)}, u32[]{:S(2)}, u32[]{:S(2)}) collective-permute-start(bf16[72,16,256]{2,1,0:T(8,128)(2,1)S(1)} %pad_maximum_fusion), channel_id=1, source_target_pairs={{0,32},{1,9},{2,34},{3,11},{4,36},{5,13},{6,38},{7,15},{8,40},{9,1... | collective-permute-start | bytes 1769480 | tf_op jit(solution)/shard_map/ppermute | solution.py:365
  16.2 3.0 %collective-permute-start.3 = (bf16[72,16,256]{2,1,0:T(8,128)(2,1)S(1)}, bf16[72,16,256]{2,1,0:T(8,128)(2,1)S(1)}, u32[]{:S(2)}, u32[]{:S(2)}) collective-permute-start(bf16[72,16,256]{2,1,0:T(8,128)(2,1)S(1)} %pad_maximum_fusion), channel_id=1, source_target_pairs={{0,4},{1,5},{2,6},{3,7},{4,0},{5,1},{6,2},{7,3},{8,12},{9,13},{10,... | collective-permute-start | bytes 1769480 | tf_op jit(solution)/shard_map/ppermute | solution.py:365
  19.2 0.7 constant_dynamic-slice_fusion
  19.9 0.1 pad_add_fusion.place_ref
  20.0 2.2 %collective-permute-start.8 = (bf16[72,16,256]{2,1,0:T(8,128)(2,1)S(1)}, bf16[72,16,256]{2,1,0:T(8,128)(2,1)S(1)}, u32[]{:S(2)}, u32[]{:S(2)}) collective-permute-start(bf16[72,16,256]{2,1,0:T(8,128)(2,1)S(1)} %pad_maximum_fusion), channel_id=1, source_target_pairs={{0,96},{1,25},{2,98},{3,27},{4,100},{5,29},{6,102},{7,31},{8,104},... | collective-permute-start | bytes 1769480 | tf_op jit(solution)/shard_map/ppermute | solution.py:365
  22.2 0.0 copy-done
  22.2 10.5 %legendre_forward.1.coeff_ref = bf16[512,32,128]{2,1,0:T(8,128)(2,1)S(1)} custom-call(s32[512]{0:T(512)S(1)} %copy-done, s32[4]{0:T(128)S(1)} %pad_add_fusion.place_ref, bf16[16,512,512]{2,1,0:T(8,128)(2,1)} %leg_ref.3, bf16[16,2,512,128]{3,2,1,0:T(8,128)(2,1)} %control_ref.3, f32[16,512]{1,0:T(8,128)} %loc_ref.3), custom_call_target="tpu_custom_call" | custom-call | flops 2147483648 | bytes 16777216 | tf_op jit(solution)/shard_map/legendre_forward/pallas_call | solution.py:127
  32.8 1.9 %collective-permute-start.7 = (bf16[72,16,256]{2,1,0:T(8,128)(2,1)S(1)}, bf16[72,16,256]{2,1,0:T(8,128)(2,1)S(1)}, u32[]{:S(2)}, u32[]{:S(2)}) collective-permute-start(bf16[72,16,256]{2,1,0:T(8,128)(2,1)S(1)} %pad_maximum_fusion), channel_id=1, source_target_pairs={{0,64},{1,17},{2,66},{3,19},{4,68},{5,21},{6,70},{7,23},{8,72},{9,... | collective-permute-start | bytes 1769480 | tf_op jit(solution)/shard_map/ppermute | solution.py:365
  34.6 2.8 %observe.8 = (bf16[1024,128]{1,0:T(8,128)(2,1)S(1)}, bf16[32,16,32,256]{3,2,1,0:T(8,128)(2,1)S(1)}, bf16[32,18,16,256]{3,2,1,0:T(8,128)(2,1)S(1)}) custom-call(s32[512]{0:T(512)S(1)} %copy-done, s32[4]{0:T(128)S(1)} %pad_add_fusion.place_ref, bf16[4,18,16,256]{3,2,1,0:T(8,128)(2,1)S(1)} %bitcast.23, bf16[512,32,128]{2,1,0:T(8,128)(2,1)S(1)} %legendre_forward.1.coeff_ref), custom_call_target="tpu_custom_call" | custom-call | flops 2400000000 | bytes 2097152 | tf_op jit(solution)/shard_map/observe/pallas_call | solution.py:222
  37.4 0.0 collective-permute-done.3
  37.5 1.1 collective-permute-start.6
  38.5 2.2 %collective-permute-start.5 = (bf16[72,16,256]{2,1,0:T(8,128)(2,1)S(1)}, bf16[72,16,256]{2,1,0:T(8,128)(2,1)S(1)}, u32[]{:S(2)}, u32[]{:S(2)}) collective-permute-start(bf16[72,16,256]{2,1,0:T(8,128)(2,1)S(1)} %collective-permute-done.3), channel_id=1, source_target_pairs={{0,96},{1,25},{2,98},{3,27},{4,100},{5,29},{6,102},{7,31},{8,104},... | collective-permute-start | bytes 1769480 | tf_op jit(solution)/shard_map/ppermute | solution.py:365
  40.8 0.0 collective-permute-done.9
  40.8 0.5 collective-permute-start.4
  41.3 2.8 %observe.9 = (bf16[1024,128]{1,0:T(8,128)(2,1)S(1)}, bf16[32,16,32,256]{3,2,1,0:T(8,128)(2,1)S(1)}, bf16[32,18,16,256]{3,2,1,0:T(8,128)(2,1)S(1)}) custom-call(s32[512]{0:T(512)S(1)} %copy-done, s32[4]{0:T(128)S(1)} %pad_add_fusion.place_ref, bf16[4,18,16,256]{3,2,1,0:T(8,128)(2,1)S(1)} %bitcast.18, ...), custom_call_target="tpu_custom_call", output_to_operand_aliasing={{0}: (4, {}), {1}: (5, {}), {2}: (6, {})} | custom-call | flops 2400000000 | bytes 2097152 | tf_op jit(solution)/shard_map/observe/pallas_call | solution.py:222
  44.1 0.0 collective-permute-done.8
  44.1 2.8 %observe.10 = (bf16[1024,128]{1,0:T(8,128)(2,1)S(1)}, bf16[32,16,32,256]{3,2,1,0:T(8,128)(2,1)S(1)}, bf16[32,18,16,256]{3,2,1,0:T(8,128)(2,1)S(1)}) custom-call(s32[512]{0:T(512)S(1)} %copy-done, s32[4]{0:T(128)S(1)} %pad_add_fusion.place_ref, bf16[4,18,16,256]{3,2,1,0:T(8,128)(2,1)S(1)} %bitcast.22, ...), custom_call_target="tpu_custom_call", output_to_operand_aliasing={{0}: (4, {}), {1}: (5, {}), {2}: (6, {})} | custom-call | flops 2400000000 | bytes 2097152 | tf_op jit(solution)/shard_map/observe/pallas_call | solution.py:222
  47.0 0.0 collective-permute-done.7
  47.0 2.8 %observe.11 = (bf16[1024,128]{1,0:T(8,128)(2,1)S(1)}, bf16[32,16,32,256]{3,2,1,0:T(8,128)(2,1)S(1)}, bf16[32,18,16,256]{3,2,1,0:T(8,128)(2,1)S(1)}) custom-call(s32[512]{0:T(512)S(1)} %copy-done, s32[4]{0:T(128)S(1)} %pad_add_fusion.place_ref, bf16[4,18,16,256]{3,2,1,0:T(8,128)(2,1)S(1)} %bitcast.21, ...), custom_call_target="tpu_custom_call", output_to_operand_aliasing={{0}: (4, {}), {1}: (5, {}), {2}: (6, {})} | custom-call | flops 2400000000 | bytes 2097152 | tf_op jit(solution)/shard_map/observe/pallas_call | solution.py:222
  49.8 2.8 %observe.12 = (bf16[1024,128]{1,0:T(8,128)(2,1)S(1)}, bf16[32,16,32,256]{3,2,1,0:T(8,128)(2,1)S(1)}, bf16[32,18,16,256]{3,2,1,0:T(8,128)(2,1)S(1)}) custom-call(s32[512]{0:T(512)S(1)} %copy-done, s32[4]{0:T(128)S(1)} %pad_add_fusion.place_ref, bf16[4,18,16,256]{3,2,1,0:T(8,128)(2,1)S(1)} %bitcast.16, ...), custom_call_target="tpu_custom_call", output_to_operand_aliasing={{0}: (4, {}), {1}: (5, {}), {2}: (6, {})} | custom-call | flops 2400000000 | bytes 2097152 | tf_op jit(solution)/shard_map/observe/pallas_call | solution.py:222
  52.6 0.0 collective-permute-done.6
  52.6 2.8 %observe.13 = (bf16[1024,128]{1,0:T(8,128)(2,1)S(1)}, bf16[32,16,32,256]{3,2,1,0:T(8,128)(2,1)S(1)}, bf16[32,18,16,256]{3,2,1,0:T(8,128)(2,1)S(1)}) custom-call(s32[512]{0:T(512)S(1)} %copy-done, s32[4]{0:T(128)S(1)} %pad_add_fusion.place_ref, bf16[4,18,16,256]{3,2,1,0:T(8,128)(2,1)S(1)} %bitcast.20, ...), custom_call_target="tpu_custom_call", output_to_operand_aliasing={{0}: (4, {}), {1}: (5, {}), {2}: (6, {})} | custom-call | flops 2400000000 | bytes 2097152 | tf_op jit(solution)/shard_map/observe/pallas_call | solution.py:222
  55.5 0.0 collective-permute-done.5
  55.5 2.8 %observe.14 = (bf16[1024,128]{1,0:T(8,128)(2,1)S(1)}, bf16[32,16,32,256]{3,2,1,0:T(8,128)(2,1)S(1)}, bf16[32,18,16,256]{3,2,1,0:T(8,128)(2,1)S(1)}) custom-call(s32[512]{0:T(512)S(1)} %copy-done, s32[4]{0:T(128)S(1)} %pad_add_fusion.place_ref, bf16[4,18,16,256]{3,2,1,0:T(8,128)(2,1)S(1)} %bitcast.19, ...), custom_call_target="tpu_custom_call", output_to_operand_aliasing={{0}: (4, {}), {1}: (5, {}), {2}: (6, {})} | custom-call | flops 2400000000 | bytes 2097152 | tf_op jit(solution)/shard_map/observe/pallas_call | solution.py:222
  58.3 0.0 collective-permute-done.4
  58.3 2.8 %observe.15 = (bf16[1024,128]{1,0:T(8,128)(2,1)S(1)}, bf16[32,16,32,256]{3,2,1,0:T(8,128)(2,1)S(1)}, bf16[32,18,16,256]{3,2,1,0:T(8,128)(2,1)S(1)}) custom-call(s32[512]{0:T(512)S(1)} %copy-done, s32[4]{0:T(128)S(1)} %pad_add_fusion.place_ref, bf16[4,18,16,256]{3,2,1,0:T(8,128)(2,1)S(1)} %bitcast.17, ...), custom_call_target="tpu_custom_call", output_to_operand_aliasing={{0}: (4, {}), {1}: (5, {}), {2}: (6, {})} | custom-call | flops 2400000000 | bytes 2097152 | tf_op jit(solution)/shard_map/observe/pallas_call | solution.py:222
  61.1 18.0 %all_to_all.10 = bf16[128,8,128]{2,1,0:T(8,128)(2,1)S(1)} all-to-all(bf16[128,8,128]{2,1,0:T(8,128)(2,1)S(1)} %bitcast.14), channel_id=1, replica_groups=mesh['wide'=32,'narrow'=4] {'wide','narrow'}, dimensions={0} | all-to-all | bytes 524288 | tf_op jit(solution)/shard_map/all_to_all | solution.py:403
  79.1 0.1 convert_reduce_fusion
  79.3 15.3 %all_to_all.11 = bf16[128,8,128]{2,1,0:T(8,128)(2,1)S(1)} all-to-all(bf16[128,8,128]{2,1,0:T(8,128)(2,1)S(1)} %broadcast_in_dim.2), channel_id=1, replica_groups=mesh['wide'=32,'narrow'=4] {'wide','narrow'}, dimensions={0} | all-to-all | bytes 524288 | tf_op jit(solution)/shard_map/all_to_all | solution.py:409
  94.6 25.4 %adjoint.1 = f32[16,2,512,128]{3,2,1,0:T(8,128)} custom-call(s32[512]{0:T(512)S(1)} %copy-done, s32[4]{0:T(128)S(1)} %pad_add_fusion.place_ref, bf16[32,18,16,256]{3,2,1,0:T(8,128)(2,1)S(1)} %get-tuple-element.53.e_ref, bf16[32,16,32,256]{3,2,1,0:T(8,128)(2,1)S(1)} %get-tuple-element.54.four_ref, bf16[1024,128]{1,0:T(8,128)(2,1)S(1)} %bitcast.15, ...), custom_call_target="tpu_custom_call" | custom-call | tf_op jit(solution)/shard_map/adjoint/pallas_call | solution.py:326
  (4 shorter events, 0.1 us)
Async XLA Ops:
  0.0 22.2 %copy-start = (s32[512]{0:T(512)S(1)}, s32[512]{0:T(512)}, u32[]{:S(2)}) copy-start(s32[512]{0:T(512)} %order_ref.19) | copy-start | bytes 6148
  4.3 6.4 %collective-permute-start = (bf16[18,16,256]{2,1,0:T(8,128)(2,1)S(1)}, bf16[18,16,256]{2,1,0:T(8,128)(2,1)S(1)}, u32[]{:S(2)}, u32[]{:S(2)}) collective-permute-start(bf16[18,16,256]{2,1,0:T(8,128)(2,1)S(1)} %pick.1), channel_id=1, source_target_pairs={{0,8},{1,33},{2,10},{3,35},{4,12},{5,37},{6,14},{7,39},{8,16},{9,4... | collective-permute-start | bytes 442376 | tf_op jit(solution)/shard_map/ppermute | solution.py:365
  6.1 7.6 %collective-permute-start.1 = (bf16[18,16,256]{2,1,0:T(8,128)(2,1)S(1)}, bf16[18,16,256]{2,1,0:T(8,128)(2,1)S(1)}, u32[]{:S(2)}, u32[]{:S(2)}) collective-permute-start(bf16[18,16,256]{2,1,0:T(8,128)(2,1)S(1)} %pick.1), channel_id=1, source_target_pairs={{0,16},{1,65},{2,18},{3,67},{4,20},{5,69},{6,22},{7,71},{8,24},{9,... | collective-permute-start | bytes 442376 | tf_op jit(solution)/shard_map/ppermute | solution.py:365
  9.0 5.1 %collective-permute-start.2 = (bf16[18,16,256]{2,1,0:T(8,128)(2,1)S(1)}, bf16[18,16,256]{2,1,0:T(8,128)(2,1)S(1)}, u32[]{:S(2)}, u32[]{:S(2)}) collective-permute-start(bf16[18,16,256]{2,1,0:T(8,128)(2,1)S(1)} %pick.1), channel_id=1, source_target_pairs={{0,24},{1,97},{2,26},{3,99},{4,28},{5,101},{6,30},{7,103},{8,0},{9... | collective-permute-start | bytes 442376 | tf_op jit(solution)/shard_map/ppermute | solution.py:365
  14.2 26.6 %collective-permute-start.9 = (bf16[72,16,256]{2,1,0:T(8,128)(2,1)S(1)}, bf16[72,16,256]{2,1,0:T(8,128)(2,1)S(1)}, u32[]{:S(2)}, u32[]{:S(2)}) collective-permute-start(bf16[72,16,256]{2,1,0:T(8,128)(2,1)S(1)} %pad_maximum_fusion), channel_id=1, source_target_pairs={{0,32},{1,9},{2,34},{3,11},{4,36},{5,13},{6,38},{7,15},{8,40},{9,1... | collective-permute-start | bytes 1769480 | tf_op jit(solution)/shard_map/ppermute | solution.py:365
  16.2 21.3 %collective-permute-start.3 = (bf16[72,16,256]{2,1,0:T(8,128)(2,1)S(1)}, bf16[72,16,256]{2,1,0:T(8,128)(2,1)S(1)}, u32[]{:S(2)}, u32[]{:S(2)}) collective-permute-start(bf16[72,16,256]{2,1,0:T(8,128)(2,1)S(1)} %pad_maximum_fusion), channel_id=1, source_target_pairs={{0,4},{1,5},{2,6},{3,7},{4,0},{5,1},{6,2},{7,3},{8,12},{9,13},{10,... | collective-permute-start | bytes 1769480 | tf_op jit(solution)/shard_map/ppermute | solution.py:365
  20.0 24.1 %collective-permute-start.8 = (bf16[72,16,256]{2,1,0:T(8,128)(2,1)S(1)}, bf16[72,16,256]{2,1,0:T(8,128)(2,1)S(1)}, u32[]{:S(2)}, u32[]{:S(2)}) collective-permute-start(bf16[72,16,256]{2,1,0:T(8,128)(2,1)S(1)} %pad_maximum_fusion), channel_id=1, source_target_pairs={{0,96},{1,25},{2,98},{3,27},{4,100},{5,29},{6,102},{7,31},{8,104},... | collective-permute-start | bytes 1769480 | tf_op jit(solution)/shard_map/ppermute | solution.py:365
  32.8 14.2 %collective-permute-start.7 = (bf16[72,16,256]{2,1,0:T(8,128)(2,1)S(1)}, bf16[72,16,256]{2,1,0:T(8,128)(2,1)S(1)}, u32[]{:S(2)}, u32[]{:S(2)}) collective-permute-start(bf16[72,16,256]{2,1,0:T(8,128)(2,1)S(1)} %pad_maximum_fusion), channel_id=1, source_target_pairs={{0,64},{1,17},{2,66},{3,19},{4,68},{5,21},{6,70},{7,23},{8,72},{9,... | collective-permute-start | bytes 1769480 | tf_op jit(solution)/shard_map/ppermute | solution.py:365
  37.5 15.2 %collective-permute-start.6 = (bf16[72,16,256]{2,1,0:T(8,128)(2,1)S(1)}, bf16[72,16,256]{2,1,0:T(8,128)(2,1)S(1)}, u32[]{:S(2)}, u32[]{:S(2)}) collective-permute-start(bf16[72,16,256]{2,1,0:T(8,128)(2,1)S(1)} %collective-permute-done.3), channel_id=1, source_target_pairs={{0,32},{1,9},{2,34},{3,11},{4,36},{5,13},{6,38},{7,15},{8,40},{9,1... | collective-permute-start | bytes 1769480 | tf_op jit(solution)/shard_map/ppermute | solution.py:365
  38.5 16.9 %collective-permute-start.5 = (bf16[72,16,256]{2,1,0:T(8,128)(2,1)S(1)}, bf16[72,16,256]{2,1,0:T(8,128)(2,1)S(1)}, u32[]{:S(2)}, u32[]{:S(2)}) collective-permute-start(bf16[72,16,256]{2,1,0:T(8,128)(2,1)S(1)} %collective-permute-done.3), channel_id=1, source_target_pairs={{0,96},{1,25},{2,98},{3,27},{4,100},{5,29},{6,102},{7,31},{8,104},... | collective-permute-start | bytes 1769480 | tf_op jit(solution)/shard_map/ppermute | solution.py:365
  40.8 17.5 %collective-permute-start.4 = (bf16[72,16,256]{2,1,0:T(8,128)(2,1)S(1)}, bf16[72,16,256]{2,1,0:T(8,128)(2,1)S(1)}, u32[]{:S(2)}, u32[]{:S(2)}) collective-permute-start(bf16[72,16,256]{2,1,0:T(8,128)(2,1)S(1)} %collective-permute-done.3), channel_id=1, source_target_pairs={{0,64},{1,17},{2,66},{3,19},{4,68},{5,21},{6,70},{7,23},{8,72},{9,... | collective-permute-start | bytes 1769480 | tf_op jit(solution)/shard_map/ppermute | solution.py:365

commit v2 on v1

--- a/solution.py
+++ b/solution.py
@@ -146,16 +146,22 @@
     )(order_map, where, in_hbm(legendre), in_hbm(control), in_hbm(loc))
 
 
-def forward_kernel(order_ref, place_ref, e_ref, coeff_ref, *rest):
+def forward_kernel(order_ref, place_ref, e0_ref, e1_ref, e2_ref, e3_ref, coeff_ref, *rest):
     part_ref, four_ref, keep_ref, lon_ref, lev_ref, ens_ref, sum_ref, turn_ref = rest[-8:]
-    hi = e_ref[0, 16].astype(jnp.float32)
-    lo = e_ref[0, 17].astype(jnp.float32)
+    part = pl.program_id(0) >> 2
+    for q, ref in enumerate((e0_ref, e1_ref, e2_ref, e3_ref)):
+
+        @pl.when(part == q)
+        def _(ref=ref):
+            keep_ref[...] = ref[...]
+
+    hi = keep_ref[0, 16].astype(jnp.float32)
+    lo = keep_ref[0, 17].astype(jnp.float32)
     low = jnp.floor(lo * (1.0 / LEVELS))
     lon_ref[...] = hi * 8.0 + low
     lev_ref[...] = lo - low * LEVELS
-    keep_ref[0] = e_ref[0]
-    members, nobs = e_ref.shape[2], e_ref.shape[3]
-    ens_ref[...] = e_ref[0, :ROWS].astype(jnp.float32)
+    members, nobs = keep_ref.shape[2], keep_ref.shape[3]
+    ens_ref[...] = keep_ref[0, :ROWS].astype(jnp.float32)
 
     @pl.when(pl.program_id(0) == 0)
     def _():
@@ -199,16 +205,18 @@
     part_ref[...] = sum_ref[...].astype(jnp.bfloat16)
 
 
-def forward(order_map, where, plane, far, e, coeff, before):
-    n = e.shape[0]
+def forward(order_map, where, plane, arrays, coeff, before):
     lats, modes, width = coeff.shape
-    nobs = e.shape[3]
+    nobs = arrays[0].shape[3]
     blocks = lats // ROWS
     lanes = nobs // 128
+    n = 4 * len(arrays)
 
     def block(i, place):
-        turn = (far - i) * place[3]
-        z, y = place[0] - far + turn, place[1] - i - turn
+        near, part = i & 3, i >> 2
+        far = part ^ (part >> 1)
+        turn = (far - near) * place[3]
+        z, y = place[0] - far + turn, place[1] - near - turn
         return (z & 3) * 8 + (y & 3) * 2 + ((place[2] + plane) & 1)
 
     e_spec = lambda f: pl.BlockSpec((1, PLANES, ROWS, nobs), f)
@@ -225,7 +233,7 @@
             num_scalar_prefetch=2,
             grid=(n,),
             in_specs=[
-                e_spec(lambda i, _, place: (i, 0, 0, 0)),
+                *[e_spec(lambda i, *_, q=q: (jnp.clip(i - 4 * q, 0, 3), 0, 0, 0)) for q in range(4)],
                 pl.BlockSpec((ROWS, modes, width), lambda i, _, place: (block(i, place), 0, 0)),
             ]
             + [pl.BlockSpec(memory_space=pl.ANY)] * len(passed),
@@ -243,13 +251,13 @@
             ],
         ),
         out_shape=out_shape,
-        input_output_aliases={4 + i: i for i in range(len(passed))},
-        compiler_params=params(6),
+        input_output_aliases={7 + i: i for i in range(len(passed))},
+        compiler_params=params(8),
         cost_estimate=pl.CostEstimate(
             flops=n * 6 * 10**8, bytes_accessed=n * 2**19, transcendentals=0
         ),
         name="observe",
-    )(order_map, where, e, coeff, *passed)
+    )(order_map, where, *arrays, coeff, *passed)
 
 
 def backward_kernel(
@@ -347,7 +355,7 @@
         out_shape=jax.ShapeDtypeStruct(control.shape, jnp.float32),
         compiler_params=params(24),
         name="adjoint",
-    )(order_map, where, e, four, misfit, in_hbm(legendre), in_hbm(control), in_hbm(loc))
+    )(order_map, where, e, four, misfit, legendre, control, in_hbm(loc))
 
 
 def send(x, distance, stage):
@@ -370,9 +378,9 @@
     near = {k: send(own, k, "near") for k in ring}
     near = jnp.concatenate([own] + [near[k] for k in (1, 2, 3)], axis=0)
     other = send(near, 1, "hop")
-    far = [(0, k, send(near, k, "far")) for k in ring]
-    across = [(1, k, send(other, k, "far")) for k in ring]
-    return [(0, 0, near)] + far + [(1, 0, other)] + across
+    far = [send(near, k, "far") for k in ring]
+    across = [send(other, k, "far") for k in ring]
+    return [near] + far, [other] + across
 
 
 def body(
@@ -388,13 +396,13 @@
     where = jnp.stack([w >> 3, (w >> 1) & 3, w & 1, n & 1]).astype(jnp.int32)
     own = pick(obs_level, obs_lon, ensemble)
 
-    blocks = gather(own)
+    planes = gather(own)
 
     coeff = legendre_forward(order_map, where, legendre, control, loc_spectrum)
     state = None
-    for plane, far, e in blocks:
-        e = e.reshape(-1, PLANES, ROWS, nobs)
-        state = forward(order_map, where, plane, far, e, coeff, state)
+    for plane, arrays in enumerate(planes):
+        arrays = [e.reshape(-1, PLANES, ROWS, nobs) for e in arrays]
+        state = forward(order_map, where, plane, arrays, coeff, state)
     part, four, e_all = state
 
     value = lax.dynamic_slice_in_dim(obs_value, n * mine, mine, 0).reshape(tile, 128)

time: 121 us -> 118 us (0.975)
  Pallas kernels: 62.7 us -> 56.1 us
  waiting for transfers between devices: 3.81 us -> 7.06 us
    pallas_call x1, Pallas kernels: 25.4 us -> 21.2 us  [backward(): pl.pallas_call(backward_kernel, grid_spec=pltpu.PrefetchScalarGridSpec(nu...]
    ppermute x10, waiting for transfers between devices: 3.81 us -> 7.06 us  [send(): return lax.ppermute(x, ('wide', 'narrow'), pairs)]
    pallas_call x8 -> x2, Pallas kernels: 22.5 us -> 20.1 us  [forward(): pl.pallas_call(forward_kernel, grid_spec=pltpu.PrefetchScalarGridSpec(num...]
  transfers between devices with their start and end apart: 10 -> 10, of which waited for: 3 -> 5; matrix products, arithmetic and copies ran while one was open for 1% -> 1% of each run, Pallas kernels for 25% -> 18%
where the time goes in v2:
time: 118 us; the launch traced here: 117 us
  Pallas kernels  56.1 us (48%)
  blocking collectives  33.7 us (29%)
  starting transfers between devices  18.8 us (16%)
  waiting for transfers between devices  7.06 us (6%)
    pallas_call x1, Pallas kernels, backward(): pl.pallas_call(backward_kernel, grid_spec=pltpu.PrefetchScalarGridSpec(nu...  21.2 us
    pallas_call x2, Pallas kernels, forward(): pl.pallas_call(forward_kernel, grid_spec=pltpu.PrefetchScalarGridSpec(num...  20.1 us
    ppermute x10, starting transfers between devices, send(): return lax.ppermute(x, ('wide', 'narrow'), pairs)  18.8 us
    all_to_all x1, blocking collectives, body(): lax.all_to_all(part.reshape(devices, tile, 128), both, split_axis=0, conc...  18.4 us
    all_to_all x1, blocking collectives, body(): lax.all_to_all(misfit, both, split_axis=0, concat_axis=0, tiled=True)  15.3 us
    pallas_call x1, Pallas kernels, legendre_forward(): pl.pallas_call(legendre_kernel, grid_spec=pltpu.PrefetchScalarGridSpec(nu...  10.5 us
    ppermute x10, waiting for transfers between devices, send(): return lax.ppermute(x, ('wide', 'narrow'), pairs)  7.06 us
    pallas_call x1, Pallas kernels, pick(): pl.pallas_call(pick_kernel, grid=(rows // PICK,), in_specs=[whole, whole,...  4.3 us
  transfers between devices with their start and end apart: 10, of which 5 were waited for; matrix products, arithmetic and copies ran while one was open for 1% of the time, Pallas kernels for 18%

profile of v2, /device:TPU:0, one launch (start us, length us, event | category | flops | bytes accessed | tf_op | source)
XLA Modules:
  0.0 116.9 jit_solution(130549884741010301)
XLA Ops:
  0.0 0.0 copy-start.1
  0.0 4.3 %pick.1 = bf16[18,16,256]{2,1,0:T(8,128)(2,1)S(1)} custom-call(s32[16,256]{1,0:T(8,128)} %level_ref.1, s32[16,256]{1,0:T(8,128)} %lon_ref.1, bf16[16,128,1024]{2,1,0:T(8,128)(2,1)} %ens_ref.1), custom_call_target="tpu_custom_call" | custom-call | tf_op jit(solution)/shard_map/pick/pallas_call | solution.py:71
  4.3 1.8 %collective-permute-start = (bf16[18,16,256]{2,1,0:T(8,128)(2,1)S(1)}, bf16[18,16,256]{2,1,0:T(8,128)(2,1)S(1)}, u32[]{:S(2)}, u32[]{:S(2)}) collective-permute-start(bf16[18,16,256]{2,1,0:T(8,128)(2,1)S(1)} %pick.1), channel_id=1, source_target_pairs={{0,8},{1,33},{2,10},{3,35},{4,12},{5,37},{6,14},{7,39},{8,16},{9,4... | collective-permute-start | bytes 442376 | tf_op jit(solution)/shard_map/ppermute | solution.py:373
  6.1 2.9 %collective-permute-start.1 = (bf16[18,16,256]{2,1,0:T(8,128)(2,1)S(1)}, bf16[18,16,256]{2,1,0:T(8,128)(2,1)S(1)}, u32[]{:S(2)}, u32[]{:S(2)}) collective-permute-start(bf16[18,16,256]{2,1,0:T(8,128)(2,1)S(1)} %pick.1), channel_id=1, source_target_pairs={{0,16},{1,65},{2,18},{3,67},{4,20},{5,69},{6,22},{7,71},{8,24},{9,... | collective-permute-start | bytes 442376 | tf_op jit(solution)/shard_map/ppermute | solution.py:373
  9.0 1.3 %collective-permute-start.2 = (bf16[18,16,256]{2,1,0:T(8,128)(2,1)S(1)}, bf16[18,16,256]{2,1,0:T(8,128)(2,1)S(1)}, u32[]{:S(2)}, u32[]{:S(2)}) collective-permute-start(bf16[18,16,256]{2,1,0:T(8,128)(2,1)S(1)} %pick.1), channel_id=1, source_target_pairs={{0,24},{1,97},{2,26},{3,99},{4,28},{5,101},{6,30},{7,103},{8,0},{9... | collective-permute-start | bytes 442376 | tf_op jit(solution)/shard_map/ppermute | solution.py:373
  10.3 0.4 collective-permute-done
  10.7 2.9 %collective-permute-done.1 = bf16[18,16,256]{2,1,0:T(8,128)(2,1)S(1)} collective-permute-done((bf16[18,16,256]{2,1,0:T(8,128)(2,1)S(1)}, bf16[18,16,256]{2,1,0:T(8,128)(2,1)S(1)}, u32[]{:S(2)}, u32[]{:S(2)}) %collective-permute-start.1) | collective-permute-done | bytes 147488 | tf_op jit(solution)/shard_map/ppermute | solution.py:373
  13.7 0.4 collective-permute-done.2
  14.1 0.1 pad_maximum_fusion
  14.2 3.1 %collective-permute-start.3 = (bf16[72,16,256]{2,1,0:T(8,128)(2,1)S(1)}, bf16[72,16,256]{2,1,0:T(8,128)(2,1)S(1)}, u32[]{:S(2)}, u32[]{:S(2)}) collective-permute-start(bf16[72,16,256]{2,1,0:T(8,128)(2,1)S(1)} %pad_maximum_fusion), channel_id=1, source_target_pairs={{0,4},{1,5},{2,6},{3,7},{4,0},{5,1},{6,2},{7,3},{8,12},{9,13},{10,... | collective-permute-start | bytes 1769480 | tf_op jit(solution)/shard_map/ppermute | solution.py:373
  17.3 4.0 %collective-permute-start.8 = (bf16[72,16,256]{2,1,0:T(8,128)(2,1)S(1)}, bf16[72,16,256]{2,1,0:T(8,128)(2,1)S(1)}, u32[]{:S(2)}, u32[]{:S(2)}) collective-permute-start(bf16[72,16,256]{2,1,0:T(8,128)(2,1)S(1)} %pad_maximum_fusion), channel_id=1, source_target_pairs={{0,96},{1,25},{2,98},{3,27},{4,100},{5,29},{6,102},{7,31},{8,104},... | collective-permute-start | bytes 1769480 | tf_op jit(solution)/shard_map/ppermute | solution.py:373
  21.3 0.0 collective-permute-start.9
  21.3 1.3 %collective-permute-start.7 = (bf16[72,16,256]{2,1,0:T(8,128)(2,1)S(1)}, bf16[72,16,256]{2,1,0:T(8,128)(2,1)S(1)}, u32[]{:S(2)}, u32[]{:S(2)}) collective-permute-start(bf16[72,16,256]{2,1,0:T(8,128)(2,1)S(1)} %pad_maximum_fusion), channel_id=1, source_target_pairs={{0,32},{1,9},{2,34},{3,11},{4,36},{5,13},{6,38},{7,15},{8,40},{9,1... | collective-permute-start | bytes 1769480 | tf_op jit(solution)/shard_map/ppermute | solution.py:373
  22.6 0.7 constant_dynamic-slice_fusion
  23.3 0.1 pad_add_fusion.place_ref
  23.4 0.0 copy-done.1
  23.4 10.5 %legendre_forward.1.coeff_ref = bf16[512,32,128]{2,1,0:T(8,128)(2,1)S(1)} custom-call(s32[512]{0:T(512)S(1)} %copy-done.1, s32[4]{0:T(128)S(1)} %pad_add_fusion.place_ref, bf16[16,512,512]{2,1,0:T(8,128)(2,1)} %leg_ref.3, bf16[16,2,512,128]{3,2,1,0:T(8,128)(2,1)} %control_ref.3, f32[16,512]{1,0:T(8,128)} %loc_ref.3), custom_call_target="tpu_custom_call" | custom-call | flops 2147483648 | bytes 16777216 | tf_op jit(solution)/shard_map/legendre_forward/pallas_call | solution.py:127
  33.9 0.0 collective-permute-done.3
  34.0 2.3 %collective-permute-start.4 = (bf16[72,16,256]{2,1,0:T(8,128)(2,1)S(1)}, bf16[72,16,256]{2,1,0:T(8,128)(2,1)S(1)}, u32[]{:S(2)}, u32[]{:S(2)}) collective-permute-start(bf16[72,16,256]{2,1,0:T(8,128)(2,1)S(1)} %collective-permute-done.3), channel_id=1, source_target_pairs={{0,32},{1,9},{2,34},{3,11},{4,36},{5,13},{6,38},{7,15},{8,40},{9,1... | collective-permute-start | bytes 1769480 | tf_op jit(solution)/shard_map/ppermute | solution.py:373
  36.2 1.0 collective-permute-start.5
  37.3 0.0 collective-permute-done.8
  37.3 1.1 collective-permute-start.6
  38.4 0.0 collective-permute-done.9
  38.4 0.3 collective-permute-done.7
  38.8 10.0 %observe.2 = (bf16[1024,128]{1,0:T(8,128)(2,1)S(1)}, bf16[32,16,32,256]{3,2,1,0:T(8,128)(2,1)S(1)}, bf16[32,18,16,256]{3,2,1,0:T(8,128)(2,1)S(1)}) custom-call(s32[512]{0:T(512)S(1)} %copy-done.1, s32[4]{0:T(128)S(1)} %pad_add_fusion.place_ref, bf16[4,18,16,256]{3,2,1,0:T(8,128)(2,1)S(1)} %bitcast.17, bf16[4,18,16,256]{3,2,1,0:T(8,128)(2,1)S(1)} %bitcast.22, ...), custom_call_target="tpu_custom_call" | custom-call | flops 9600000000 | bytes 8388608 | tf_op jit(solution)/shard_map/observe/pallas_call | solution.py:230
  48.8 0.0 collective-permute-done.4
  48.8 0.0 collective-permute-done.5
  48.8 2.9 %collective-permute-done.6 = bf16[72,16,256]{2,1,0:T(8,128)(2,1)S(1)} collective-permute-done((bf16[72,16,256]{2,1,0:T(8,128)(2,1)S(1)}, bf16[72,16,256]{2,1,0:T(8,128)(2,1)S(1)}, u32[]{:S(2)}, u32[]{:S(2)}) %collective-permute-start.6) | collective-permute-done | bytes 589856 | tf_op jit(solution)/shard_map/ppermute | solution.py:373
  51.7 0.0 slice-start
  51.7 0.0 slice-start.1
  51.7 0.0 copy-start
  51.7 10.1 %observe.3 = (bf16[1024,128]{1,0:T(8,128)(2,1)S(1)}, bf16[32,16,32,256]{3,2,1,0:T(8,128)(2,1)S(1)}, bf16[32,18,16,256]{3,2,1,0:T(8,128)(2,1)S(1)}) custom-call(s32[512]{0:T(512)S(1)} %copy-done.1, s32[4]{0:T(128)S(1)} %pad_add_fusion.place_ref, bf16[4,18,16,256]{3,2,1,0:T(8,128)(2,1)S(1)} %bitcast.19, ...), custom_call_target="tpu_custom_call", output_to_operand_aliasing={{0}: (7, {}), {1}: (8, {}), {2}: (9, {})} | custom-call | flops 9600000000 | bytes 8388608 | tf_op jit(solution)/shard_map/observe/pallas_call | solution.py:230
  61.8 18.4 %all_to_all.10 = bf16[128,8,128]{2,1,0:T(8,128)(2,1)S(1)} all-to-all(bf16[128,8,128]{2,1,0:T(8,128)(2,1)S(1)} %bitcast.18), channel_id=1, replica_groups=mesh['wide'=32,'narrow'=4] {'wide','narrow'}, dimensions={0} | all-to-all | bytes 524288 | tf_op jit(solution)/shard_map/all_to_all | solution.py:411
  80.2 0.1 convert_reduce_fusion
  80.4 15.3 %all_to_all.11 = bf16[128,8,128]{2,1,0:T(8,128)(2,1)S(1)} all-to-all(bf16[128,8,128]{2,1,0:T(8,128)(2,1)S(1)} %broadcast_in_dim.2), channel_id=1, replica_groups=mesh['wide'=32,'narrow'=4] {'wide','narrow'}, dimensions={0} | all-to-all | bytes 524288 | tf_op jit(solution)/shard_map/all_to_all | solution.py:417
  95.7 0.0 slice-done
  95.7 0.0 slice-done.1
  95.7 0.0 copy-done
  95.7 21.2 %adjoint.1 = f32[16,2,512,128]{3,2,1,0:T(8,128)} custom-call(s32[512]{0:T(512)S(1)} %copy-done.1, s32[4]{0:T(128)S(1)} %pad_add_fusion.place_ref, bf16[32,18,16,256]{3,2,1,0:T(8,128)(2,1)S(1)} %get-tuple-element.17.e_ref, bf16[32,16,32,256]{3,2,1,0:T(8,128)(2,1)S(1)} %get-tuple-element.18.four_ref, bf16[1024,128]{1,0:T(8,128)(2,1)S(1)} %bitcast.16, ...), custom_call_target="tpu_custom_call" | custom-call | tf_op jit(solution)/shard_map/adjoint/pallas_call | solution.py:334
  (5 shorter events, 0.1 us)
Async XLA Ops:
  0.0 23.4 %copy-start.1 = (s32[512]{0:T(512)S(1)}, s32[512]{0:T(512)}, u32[]{:S(2)}) copy-start(s32[512]{0:T(512)} %order_ref.7) | copy-start | bytes 6148
  4.3 6.4 %collective-permute-start = (bf16[18,16,256]{2,1,0:T(8,128)(2,1)S(1)}, bf16[18,16,256]{2,1,0:T(8,128)(2,1)S(1)}, u32[]{:S(2)}, u32[]{:S(2)}) collective-permute-start(bf16[18,16,256]{2,1,0:T(8,128)(2,1)S(1)} %pick.1), channel_id=1, source_target_pairs={{0,8},{1,33},{2,10},{3,35},{4,12},{5,37},{6,14},{7,39},{8,16},{9,4... | collective-permute-start | bytes 442376 | tf_op jit(solution)/shard_map/ppermute | solution.py:373
  6.1 7.6 %collective-permute-start.1 = (bf16[18,16,256]{2,1,0:T(8,128)(2,1)S(1)}, bf16[18,16,256]{2,1,0:T(8,128)(2,1)S(1)}, u32[]{:S(2)}, u32[]{:S(2)}) collective-permute-start(bf16[18,16,256]{2,1,0:T(8,128)(2,1)S(1)} %pick.1), channel_id=1, source_target_pairs={{0,16},{1,65},{2,18},{3,67},{4,20},{5,69},{6,22},{7,71},{8,24},{9,... | collective-permute-start | bytes 442376 | tf_op jit(solution)/shard_map/ppermute | solution.py:373
  9.0 5.1 %collective-permute-start.2 = (bf16[18,16,256]{2,1,0:T(8,128)(2,1)S(1)}, bf16[18,16,256]{2,1,0:T(8,128)(2,1)S(1)}, u32[]{:S(2)}, u32[]{:S(2)}) collective-permute-start(bf16[18,16,256]{2,1,0:T(8,128)(2,1)S(1)} %pick.1), channel_id=1, source_target_pairs={{0,24},{1,97},{2,26},{3,99},{4,28},{5,101},{6,30},{7,103},{8,0},{9... | collective-permute-start | bytes 442376 | tf_op jit(solution)/shard_map/ppermute | solution.py:373
  14.2 19.7 %collective-permute-start.3 = (bf16[72,16,256]{2,1,0:T(8,128)(2,1)S(1)}, bf16[72,16,256]{2,1,0:T(8,128)(2,1)S(1)}, u32[]{:S(2)}, u32[]{:S(2)}) collective-permute-start(bf16[72,16,256]{2,1,0:T(8,128)(2,1)S(1)} %pad_maximum_fusion), channel_id=1, source_target_pairs={{0,4},{1,5},{2,6},{3,7},{4,0},{5,1},{6,2},{7,3},{8,12},{9,13},{10,... | collective-permute-start | bytes 1769480 | tf_op jit(solution)/shard_map/ppermute | solution.py:373
  17.3 20.0 %collective-permute-start.8 = (bf16[72,16,256]{2,1,0:T(8,128)(2,1)S(1)}, bf16[72,16,256]{2,1,0:T(8,128)(2,1)S(1)}, u32[]{:S(2)}, u32[]{:S(2)}) collective-permute-start(bf16[72,16,256]{2,1,0:T(8,128)(2,1)S(1)} %pad_maximum_fusion), channel_id=1, source_target_pairs={{0,96},{1,25},{2,98},{3,27},{4,100},{5,29},{6,102},{7,31},{8,104},... | collective-permute-start | bytes 1769480 | tf_op jit(solution)/shard_map/ppermute | solution.py:373
  21.3 17.1 %collective-permute-start.9 = (bf16[72,16,256]{2,1,0:T(8,128)(2,1)S(1)}, bf16[72,16,256]{2,1,0:T(8,128)(2,1)S(1)}, u32[]{:S(2)}, u32[]{:S(2)}) collective-permute-start(bf16[72,16,256]{2,1,0:T(8,128)(2,1)S(1)} %pad_maximum_fusion), channel_id=1, source_target_pairs={{0,64},{1,17},{2,66},{3,19},{4,68},{5,21},{6,70},{7,23},{8,72},{9,... | collective-permute-start | bytes 1769480 | tf_op jit(solution)/shard_map/ppermute | solution.py:373
  21.3 17.4 %collective-permute-start.7 = (bf16[72,16,256]{2,1,0:T(8,128)(2,1)S(1)}, bf16[72,16,256]{2,1,0:T(8,128)(2,1)S(1)}, u32[]{:S(2)}, u32[]{:S(2)}) collective-permute-start(bf16[72,16,256]{2,1,0:T(8,128)(2,1)S(1)} %pad_maximum_fusion), channel_id=1, source_target_pairs={{0,32},{1,9},{2,34},{3,11},{4,36},{5,13},{6,38},{7,15},{8,40},{9,1... | collective-permute-start | bytes 1769480 | tf_op jit(solution)/shard_map/ppermute | solution.py:373
  34.0 14.8 %collective-permute-start.4 = (bf16[72,16,256]{2,1,0:T(8,128)(2,1)S(1)}, bf16[72,16,256]{2,1,0:T(8,128)(2,1)S(1)}, u32[]{:S(2)}, u32[]{:S(2)}) collective-permute-start(bf16[72,16,256]{2,1,0:T(8,128)(2,1)S(1)} %collective-permute-done.3), channel_id=1, source_target_pairs={{0,32},{1,9},{2,34},{3,11},{4,36},{5,13},{6,38},{7,15},{8,40},{9,1... | collective-permute-start | bytes 1769480 | tf_op jit(solution)/shard_map/ppermute | solution.py:373
  36.2 12.6 %collective-permute-start.5 = (bf16[72,16,256]{2,1,0:T(8,128)(2,1)S(1)}, bf16[72,16,256]{2,1,0:T(8,128)(2,1)S(1)}, u32[]{:S(2)}, u32[]{:S(2)}) collective-permute-start(bf16[72,16,256]{2,1,0:T(8,128)(2,1)S(1)} %collective-permute-done.3), channel_id=1, source_target_pairs={{0,96},{1,25},{2,98},{3,27},{4,100},{5,29},{6,102},{7,31},{8,104},... | collective-permute-start | bytes 1769480 | tf_op jit(solution)/shard_map/ppermute | solution.py:373
  37.3 14.5 %collective-permute-start.6 = (bf16[72,16,256]{2,1,0:T(8,128)(2,1)S(1)}, bf16[72,16,256]{2,1,0:T(8,128)(2,1)S(1)}, u32[]{:S(2)}, u32[]{:S(2)}) collective-permute-start(bf16[72,16,256]{2,1,0:T(8,128)(2,1)S(1)} %collective-permute-done.3), channel_id=1, source_target_pairs={{0,64},{1,17},{2,66},{3,19},{4,68},{5,21},{6,70},{7,23},{8,72},{9,... | collective-permute-start | bytes 1769480 | tf_op jit(solution)/shard_map/ppermute | solution.py:373
  51.7 44.0 %slice-start = ((s8[8388608]{0:T(1024)(128)(4,1)}), s8[4194304]{0:T(1024)(128)(4,1)S(1)}, s32[]{:S(2)}) async-start(s8[8388608]{0:T(1024)(128)(4,1)} %bitcast.14), calls=%async_computation.2 | async-start | bytes 8388608
  51.7 44.0 %slice-start.1 = ((s8[8388608]{0:T(1024)(128)(4,1)}), s8[4194304]{0:T(1024)(128)(4,1)S(1)}, s32[]{:S(2)}) async-start(s8[8388608]{0:T(1024)(128)(4,1)} %bitcast.14), calls=%async_computation.3 | async-start | bytes 8388608
  51.7 44.0 %copy-start = (bf16[16,2,512,128]{3,2,1,0:T(8,128)(2,1)S(1)}, bf16[16,2,512,128]{3,2,1,0:T(8,128)(2,1)}, u32[]{:S(2)}) copy-start(bf16[16,2,512,128]{3,2,1,0:T(8,128)(2,1)} %control_ref.3) | copy-start | bytes 12582916
